TPU v7x, 256 devices: a whole 4x4x8 slice. The times are simulated.
256 devices in a mesh: row: 16 (over z, core), col: 16 (over y, x).
Axes of the slice: x: 4, y: 4, z: 8, core: 2. Of those that a mesh axis runs over, the one named last changes fastest.
Arguments:
- points: float32 [32, 65536], P(None, ('row', 'col')), may hold values from -6 to 6
- search: float32 [96, 65536], P(None, ('row', 'col')), may hold values from -24 to 24
Outputs:
- applied: float32 [96, 65536], P(None, ('row', 'col'))
- gram_a: float32 [96, 96], replicated
- gram_b: float32 [96, 96], replicated
- q_block: float32 [32, 65536], P(None, ('row', 'col'))
All inputs are finite; a program needn't handle non-finite values.
Results may differ from a plain program's by a relative error of at most 0.00036.
Values may be sent and summed in bfloat16 or wider, within the bound.
A program may use at most 128 MiB of HBM per device.

v0:
```python
import jax
import jax.numpy as jnp
from jax import lax
from jax.sharding import PartitionSpec as P

NEV = 32


def step_width():
    return 256


def pair_tile(source_points, source_squares, target_points, target_squares, kernel_rate):
    cross_terms = lax.dot_general(
        source_points,
        target_points,
        (((0,), (0,)), ((), ())),
        precision=lax.Precision.HIGHEST,
        preferred_element_type=jnp.float32,
    )
    return jnp.exp(
        -kernel_rate * (source_squares[:, None] + target_squares[None, :] - 2.0 * cross_terms)
    )


def degree_stored(source_points, source_squares, target_points, target_squares, kernel_rate):
    span_width = source_points.shape[1]
    stride = step_width()

    def degree_add_block(step_index, carry):
        running, stored = carry
        offset = step_index * stride
        block_points = lax.dynamic_slice_in_dim(source_points, offset, stride, 1)
        block_squares = lax.dynamic_slice_in_dim(source_squares, offset, stride, 0)
        affinity = pair_tile(
            block_points, block_squares, target_points, target_squares, kernel_rate
        )
        stored = lax.dynamic_update_slice_in_dim(stored, affinity.astype(jnp.bfloat16), offset, 0)
        return (running + jnp.sum(affinity, axis=0), stored)

    zero_sums = jnp.zeros((target_points.shape[1],), jnp.float32)
    empty_tile = jnp.zeros((span_width, target_points.shape[1]), jnp.bfloat16)
    return lax.fori_loop(0, span_width // stride, degree_add_block, (zero_sums, empty_tile))


def fold_stored(stored):

    def accumulate(running, shard_piece, first_index):
        span_width = shard_piece.shape[1]
        stride = step_width()

        def accumulate_add_block(step_index, partial_value):
            offset = step_index * stride
            columns = lax.dynamic_slice_in_dim(shard_piece, offset, stride, 1)
            tile_rows = lax.dynamic_slice_in_dim(stored, offset, stride, 0)
            return partial_value + jnp.dot(columns, tile_rows, preferred_element_type=jnp.float32)

        return lax.fori_loop(0, span_width // stride, accumulate_add_block, running)

    return accumulate


def degrees_and_fold(source_points, target_points, kernel_rate):
    target_squares = jnp.sum(target_points * target_points, axis=0)
    source_squares = jnp.sum(source_points * source_points, axis=0)
    partial_value, stored = degree_stored(
        source_points, source_squares, target_points, target_squares, kernel_rate
    )
    accumulate = fold_stored(stored)
    return (partial_value, accumulate)


def per_device(points, search):
    kernel_rate = 2.0 / points.shape[0]
    target_points = lax.all_gather(points, "col", axis=1, tiled=True)
    source_points = lax.all_gather(points, "row", axis=1, tiled=True)
    partial_value, accumulate = degrees_and_fold(source_points, target_points, kernel_rate)
    degrees = lax.psum_scatter(partial_value, "col", scatter_dimension=0, tiled=True)
    inverse_root = lax.rsqrt(degrees)
    scaled = (search * inverse_root[None, :]).astype(jnp.bfloat16)
    zero_sums = jnp.zeros((search.shape[0], target_points.shape[1]), jnp.float32)
    totals = accumulate(zero_sums, lax.all_gather(scaled, "row", axis=1, tiled=True), jnp.int32(0))
    applied = (
        lax.psum_scatter(totals, "col", scatter_dimension=1, tiled=True) * inverse_root[None, :]
    )
    point_count = search.shape[1] * lax.axis_size("row") * lax.axis_size("col")
    contract = (((1,), (1,)), ((), ()))
    local_a = lax.dot_general(
        search,
        applied,
        contract,
        precision=lax.Precision.HIGHEST,
        preferred_element_type=jnp.float32,
    )
    local_b = lax.dot_general(
        search,
        search,
        contract,
        precision=lax.Precision.HIGHEST,
        preferred_element_type=jnp.float32,
    )
    sum_a, sum_b = lax.psum((local_a, local_b), ("row", "col"))
    gram_a = sum_a / point_count
    gram_b = sum_b / point_count
    factor_b = jnp.linalg.cholesky(gram_b[:NEV, :NEV])
    mapping = jax.scipy.linalg.cho_solve((factor_b, True), gram_a[:NEV, :NEV]).T
    residual = applied[:NEV] - jnp.dot(mapping, search[:NEV], precision=lax.Precision.HIGHEST)
    local_r = lax.dot_general(
        residual,
        residual,
        contract,
        precision=lax.Precision.HIGHEST,
        preferred_element_type=jnp.float32,
    )
    residual_gram = lax.psum(local_r, ("row", "col")) / point_count
    factor_r = jnp.linalg.cholesky(residual_gram)
    q_block = jax.scipy.linalg.solve_triangular(factor_r, residual, lower=True)
    return (applied, gram_a, gram_b, q_block)


def solution(mesh):
    placed = (P(None, ("row", "col")), P(None, ("row", "col")))
    return jax.shard_map(
        per_device,
        mesh=mesh,
        in_specs=placed,
        out_specs=(P(None, ("row", "col")), P(), P(), P(None, ("row", "col"))),
        check_vma=False,
    )
```

profile of v0, /device:TPU:1, one launch (start us, length us, event | category | flops | bytes accessed | tf_op | source)
XLA Modules:
  0.0 711.1 jit_solution(5972083221102079643)
XLA Ops:
  7.2 20.0 %all_gather.10 = f32[32,4096]{1,0:T(8,128)S(1)} all-gather(f32[32,256]{1,0:T(8,128)} %param.7), channel_id=1, replica_groups=mesh['row'=16,'col'=16] {'col'}, dimensions={1}, use_global_device_ids=true | all-gather | bytes 557056 | tf_op jit(solution)/shard_map/all_gather | solution.py:75
  27.2 27.3 %all_gather.9 = f32[32,4096]{1,0:T(8,128)S(1)} all-gather(f32[32,256]{1,0:T(8,128)} %param.7), channel_id=1, replica_groups=mesh['row'=16,'col'=16] {'row'}, dimensions={1}, use_global_device_ids=true | all-gather | bytes 557056 | tf_op jit(solution)/shard_map/all_gather | solution.py:76
  54.6 11.0 %broadcast_in_dim.20 = bf16[4096,4096]{1,0:T(8,128)(2,1)} broadcast(bf16[]{:T(256)} %constant.130.clone.1), dimensions={} | broadcast | bytes 33554432 | tf_op jit(solution)/shard_map/broadcast_in_dim | solution.py:42
  65.6 98.8 %while.30 = (s32[]{:T(128)}, f32[4096]{0:T(1024)S(1)}, bf16[4096,4096]{1,0:T(8,128)(2,1)}, f32[4096]{0:T(1024)S(1)}, f32[4096]{0:T(1024)S(1)}, /*index=5*/f32[32...) while((s32[]{:T(128)}, f32[4096]{0:T(1024)S(1)}, ...), condition=%wide.region_4.0_spmd.clone, body=%wide.region_2.0_spmd.clone.sunk | while | flops 408948736 | bytes 6933681 | solution.py:43
  65.6 4.6 fusion.40
  71.8 4.6 fusion.40
  78.0 4.6 fusion.40
  84.1 4.6 fusion.40
  96.5 4.6 fusion.40
  102.7 4.6 fusion.40
  108.9 4.6 fusion.40
  115.0 4.6 fusion.40
  121.2 4.6 fusion.40
  127.4 4.6 fusion.40
  133.5 4.6 fusion.40
  139.7 4.6 fusion.40
  145.9 4.6 fusion.40
  158.3 4.6 fusion.40
  164.3 58.1 %all-reduce = f32[4096]{0:T(1024)S(1)} all-reduce(f32[4096]{0:T(1024)S(1)} %get-tuple-element.209), channel_id=2, replica_groups=mesh['row'=16,'col'=16] {'col'}, use_global_device_ids=true, to_apply=%region_5.0.clone | all-reduce | flops 4096 | bytes 32768
  223.8 30.7 %all_gather.11 = bf16[96,4096]{1,0:T(8,128)(2,1)S(1)} all-gather(bf16[96,256]{1,0:T(8,128)(2,1)S(1)} %multiply_convert_fusion), channel_id=1, replica_groups=mesh['row'=16,'col'=16] {'row'}, dimensions={1}, use_global_device_ids=true | all-gather | bytes 835584 | tf_op jit(solution)/shard_map/all_gather | solution.py:82
  254.5 38.2 %while.31 = (s32[]{:T(128)}, f32[96,4096]{1,0:T(8,128)S(1)}, bf16[96,4096]{1,0:T(8,128)(2,1)S(1)}, bf16[4096,4096]{1,0:T(8,128)(2,1)}, s32[]{:T(128)}, /*index=5*/s32[]{:T(128)}, s32[]{:T(128)}, s32[]{:T(128)}) while((s32[]{:T(128)}, f32[96,4096]{1,0:T(8,128)S(1)}, bf16[96,4096]{1,0:T(8,128)(2,1)S(1)}, ...), condition=%wide.region_7.0_spmd.clone, body=%wide.region_6.0_spmd.clone.sunk | while | flops 202113024 | bytes 5293708 | solution.py:58
  294.8 69.3 %reduce-scatter.2.cloned.1.call-done = f32[96,256]{1,0:T(8,128)} async-done(((f32[96,4096]{1,0:T(8,128)}), f32[96,256]{1,0:T(8,128)}) %reduce-scatter.2.cloned.1.call-update) | async-done | bytes 98320 | tf_op jit(solution)/shard_map/reduce_scatter | solution.py:84
  365.9 246.6 %all-reduce.4.cloned.1.call-done = (f32[96,96]{0,1:T(8,128)}, f32[96,96]{0,1:T(8,128)}) async-done(((f32[96,96]{0,1:T(8,128)}, f32[96,96]{0,1:T(8,128)}), (f32[96,96]{0,1:T(8,128)}, f32[96,96]{0,1:T(8,128)})) %all-reduce.4.cloned.1.call-update) | async-done | bytes 73744 | tf_op jit(solution)/shard_map/psum | solution.py:102
  622.3 74.3 %psum.23 = f32[32,32]{0,1:T(8,128)S(1)} all-reduce(f32[32,32]{0,1:T(8,128)S(1)} %fusion.24), channel_id=1, replica_groups=mesh['row'=16,'col'=16] {'row','col'}, use_global_device_ids=true, to_apply=%region_13.15 | all-reduce | flops 1024 | bytes 8192 | tf_op jit(solution)/shard_map/psum | solution.py:115
  (112 shorter events, 93.9 us)
Async XLA Ops:
  7.2 356.9 %reduce-scatter.2.cloned.1.call-start = ((), (), s32[]{:S(2)}) async-start(), calls=%async_computation.1 | async-start | bytes 1671168 | tf_op jit(solution)/shard_map/reduce_scatter | solution.py:84
  65.6 156.9 %copy-start.3 = (u32[256]{0:T(256)S(1)}, u32[256]{0:T(256)}, u32[]{:S(2)}) copy-start(u32[256]{0:T(256)} %constant.134) | copy-start | bytes 3076
  65.6 158.2 %copy-start.1 = (f32[96,256]{1,0:T(8,128)S(1)}, f32[96,256]{1,0:T(8,128)}, u32[]{:S(2)}) copy-start(f32[96,256]{1,0:T(8,128)} %param.8) | copy-start | bytes 294916
  292.7 1.2 copy-start
  293.9 318.6 %all-reduce.4.cloned.1.call-start = ((), (), s32[]{:S(2)}) async-start(), calls=%async_computation.2 | async-start | bytes 196608 | tf_op jit(solution)/shard_map/psum | solution.py:102
  365.0 339.3 %copy-start.2 = (f32[96,256]{1,0:T(8,128)}, f32[96,256]{1,0:T(8,128)S(1)}, u32[]{:S(2)}) copy-start(f32[96,256]{1,0:T(8,128)S(1)} %broadcast_multiply_fusion) | copy-start | bytes 294916
Sparse Core Ops, SparseCore 0:
  294.0 70.0 reduce-scatter.1
  370.3 242.1 all-reduce.3
where the time goes:
time: 712 us; the launch traced here: 711 us
  waiting for transfers between devices  316 us (44%)
  blocking collectives  210 us (29%)
  matrix products  115 us (16%)
  local copies, waits for them, and re-layouts  39.2 us (6%)
  other arithmetic  15.3 us (2%)
  between operations  14.8 us (2%)
    psum x1, waiting for transfers between devices, per_device(): sum_a, sum_b = lax.psum((local_a, local_b), ('row', 'col'))  247 us
    psum x1, blocking collectives, per_device(): residual_gram = lax.psum(local_r, ('row', 'col')) / point_count  74.3 us
    dot_general x16, matrix products, pair_tile(): lax.dot_general(source_points, target_points, (((0,), (0,)), ((), ())), p...  73.7 us
    reduce_scatter x1, waiting for transfers between devices, per_device(): lax.psum_scatter(totals, 'col', scatter_dimension=1, tiled=True)  69.3 us
    unnamed x1, blocking collectives  58.1 us
    dot_general x16, matrix products, accumulate_add_block(): jnp.dot(columns, tile_rows, preferred_element_type=jnp.float32)  37.7 us
    all_gather x1, blocking collectives, per_device(): lax.all_gather(scaled, 'row', axis=1, tiled=True)  30.7 us
    all_gather x1, blocking collectives, per_device(): source_points = lax.all_gather(points, 'row', axis=1, tiled=True)  27.3 us
  transfers between devices with their start and end apart: 2, of which 2 were waited for; matrix products, arithmetic and copies ran while one was open for 0% of the time, Pallas kernels for 0%

commit v1 on v0

--- a/solution.py
+++ b/solution.py
@@ -1,9 +1,19 @@
+import functools
 import jax
 import jax.numpy as jnp
 from jax import lax
 from jax.sharding import PartitionSpec as P
 
 NEV = 32
+
+
+def run_windows_on_mesh(mine, dev_axis, device_axis):
+    for rr in (dev_axis, device_axis):
+        mine = lax.psum(mine, rr)
+    return mine
+
+
+track_sizes_in = functools.partial(run_windows_on_mesh, dev_axis="col", device_axis="row")
 
 
 def step_width():
@@ -99,7 +109,7 @@
         precision=lax.Precision.HIGHEST,
         preferred_element_type=jnp.float32,
     )
-    sum_a, sum_b = lax.psum((local_a, local_b), ("row", "col"))
+    sum_a, sum_b = track_sizes_in((local_a, local_b))
     gram_a = sum_a / point_count
     gram_b = sum_b / point_count
     factor_b = jnp.linalg.cholesky(gram_b[:NEV, :NEV])

time: 712 us -> 668 us (0.938)
  waiting for transfers between devices: 316 us -> 270 us
    psum x1 -> x2, waiting for transfers between devices: 247 us -> 201 us  [run_windows_on_mesh(): mine = lax.psum(mine, rr)]
  transfers between devices with their start and end apart: 2 -> 3, of which waited for: 2 -> 3; matrix products, arithmetic and copies ran while one was open for 0% -> 0% of each run, Pallas kernels for 0% -> 0%
where the time goes in v1:
time: 668 us; the launch traced here: 667 us
  waiting for transfers between devices  270 us (40%)
  blocking collectives  213 us (32%)
  matrix products  115 us (17%)
  local copies, waits for them, and re-layouts  39.2 us (6%)
  other arithmetic  15.3 us (2%)
  between operations  14.5 us (2%)
    psum x2, waiting for transfers between devices, run_windows_on_mesh(): mine = lax.psum(mine, rr)  201 us
    psum x1, blocking collectives, per_device(): residual_gram = lax.psum(local_r, ('row', 'col')) / point_count  76.5 us
    dot_general x16, matrix products, pair_tile(): lax.dot_general(source_points, target_points, (((0,), (0,)), ((), ())), p...  73.7 us
    reduce_scatter x1, waiting for transfers between devices, per_device(): lax.psum_scatter(totals, 'col', scatter_dimension=1, tiled=True)  69.3 us
    unnamed x1, blocking collectives  58.1 us
    dot_general x16, matrix products, accumulate_add_block(): jnp.dot(columns, tile_rows, preferred_element_type=jnp.float32)  37.7 us
    all_gather x1, blocking collectives, per_device(): lax.all_gather(scaled, 'row', axis=1, tiled=True)  30.7 us
    all_gather x1, blocking collectives, per_device(): source_points = lax.all_gather(points, 'row', axis=1, tiled=True)  27.3 us
  transfers between devices with their start and end apart: 3, of which 3 were waited for; matrix products, arithmetic and copies ran while one was open for 0% of the time, Pallas kernels for 0%

profile of v1, /device:TPU:1, one launch (start us, length us, event | category | flops | bytes accessed | tf_op | source)
XLA Modules:
  0.0 667.4 jit_solution(14540982678470360163)
XLA Ops:
  7.2 20.0 %all_gather.10 = f32[32,4096]{1,0:T(8,128)S(1)} all-gather(f32[32,256]{1,0:T(8,128)} %param.7), channel_id=1, replica_groups=mesh['row'=16,'col'=16] {'col'}, dimensions={1}, use_global_device_ids=true | all-gather | bytes 557056 | tf_op jit(solution)/shard_map/all_gather | solution.py:85
  27.2 27.3 %all_gather.9 = f32[32,4096]{1,0:T(8,128)S(1)} all-gather(f32[32,256]{1,0:T(8,128)} %param.7), channel_id=1, replica_groups=mesh['row'=16,'col'=16] {'row'}, dimensions={1}, use_global_device_ids=true | all-gather | bytes 557056 | tf_op jit(solution)/shard_map/all_gather | solution.py:86
  54.6 11.0 %broadcast_in_dim.20 = bf16[4096,4096]{1,0:T(8,128)(2,1)} broadcast(bf16[]{:T(256)} %constant.130.clone.1), dimensions={} | broadcast | bytes 33554432 | tf_op jit(solution)/shard_map/broadcast_in_dim | solution.py:52
  65.6 98.8 %while.30 = (s32[]{:T(128)}, f32[4096]{0:T(1024)S(1)}, bf16[4096,4096]{1,0:T(8,128)(2,1)}, f32[4096]{0:T(1024)S(1)}, f32[4096]{0:T(1024)S(1)}, /*index=5*/f32[32...) while((s32[]{:T(128)}, f32[4096]{0:T(1024)S(1)}, ...), condition=%wide.region_4.0_spmd.clone, body=%wide.region_2.0_spmd.clone.sunk | while | flops 408948736 | bytes 6933681 | solution.py:53
  65.6 4.6 fusion.40
  71.8 4.6 fusion.40
  78.0 4.6 fusion.40
  84.1 4.6 fusion.40
  96.5 4.6 fusion.40
  108.9 4.6 fusion.40
  115.0 4.6 fusion.40
  121.2 4.6 fusion.40
  127.4 4.6 fusion.40
  133.5 4.6 fusion.40
  139.7 4.6 fusion.40
  145.9 4.6 fusion.40
  158.3 4.6 fusion.40
  164.3 58.1 %all-reduce = f32[4096]{0:T(1024)S(1)} all-reduce(f32[4096]{0:T(1024)S(1)} %get-tuple-element.209), channel_id=2, replica_groups=mesh['row'=16,'col'=16] {'col'}, use_global_device_ids=true, to_apply=%region_5.0.clone | all-reduce | flops 4096 | bytes 32768
  223.8 30.7 %all_gather.11 = bf16[96,4096]{1,0:T(8,128)(2,1)S(1)} all-gather(bf16[96,256]{1,0:T(8,128)(2,1)S(1)} %multiply_convert_fusion), channel_id=1, replica_groups=mesh['row'=16,'col'=16] {'row'}, dimensions={1}, use_global_device_ids=true | all-gather | bytes 835584 | tf_op jit(solution)/shard_map/all_gather | solution.py:92
  254.5 38.2 %while.31 = (s32[]{:T(128)}, f32[96,4096]{1,0:T(8,128)S(1)}, bf16[96,4096]{1,0:T(8,128)(2,1)S(1)}, bf16[4096,4096]{1,0:T(8,128)(2,1)}, s32[]{:T(128)}, /*index=5*/s32[]{:T(128)}, s32[]{:T(128)}, s32[]{:T(128)}) while((s32[]{:T(128)}, f32[96,4096]{1,0:T(8,128)S(1)}, bf16[96,4096]{1,0:T(8,128)(2,1)S(1)}, ...), condition=%wide.region_7.0_spmd.clone, body=%wide.region_6.0_spmd.clone.sunk | while | flops 202113024 | bytes 5293708 | solution.py:68
  294.8 69.3 %reduce-scatter.2.cloned.1.call-done = f32[96,256]{1,0:T(8,128)} async-done(((f32[96,4096]{1,0:T(8,128)}), f32[96,256]{1,0:T(8,128)}) %reduce-scatter.2.cloned.1.call-update) | async-done | bytes 98320 | tf_op jit(solution)/shard_map/reduce_scatter | solution.py:94
  365.9 93.7 %all-reduce.6.cloned.1.call-done = (f32[96,96]{0,1:T(8,128)}, f32[96,96]{0,1:T(8,128)}) async-done(((f32[96,96]{0,1:T(8,128)}, f32[96,96]{0,1:T(8,128)}), (f32[96,96]{0,1:T(8,128)}, f32[96,96]{0,1:T(8,128)})) %all-reduce.6.cloned.1.call-update) | async-done | bytes 73744 | tf_op jit(solution)/shard_map/psum | solution.py:12
  459.6 107.3 %all-reduce.8.cloned.1.call-done = (f32[96,96]{0,1:T(8,128)}, f32[96,96]{0,1:T(8,128)}) async-done(((f32[96,96]{0,1:T(8,128)}, f32[96,96]{0,1:T(8,128)}), (f32[96,96]{0,1:T(8,128)}, f32[96,96]{0,1:T(8,128)})) %all-reduce.8.cloned.1.call-update) | async-done | bytes 73744 | tf_op jit(solution)/shard_map/psum | solution.py:12
  576.7 76.5 %psum.39 = f32[32,32]{0,1:T(8,128)S(1)} all-reduce(f32[32,32]{0,1:T(8,128)S(1)} %fusion.24), channel_id=1, replica_groups=mesh['row'=16,'col'=16] {'row','col'}, use_global_device_ids=true, to_apply=%region_15.17 | all-reduce | flops 1024 | bytes 8192 | tf_op jit(solution)/shard_map/psum | solution.py:125
  (115 shorter events, 98.6 us)
Async XLA Ops:
  7.2 356.9 %reduce-scatter.2.cloned.1.call-start = ((), (), s32[]{:S(2)}) async-start(), calls=%async_computation.1 | async-start | bytes 1671168 | tf_op jit(solution)/shard_map/reduce_scatter | solution.py:94
  65.6 156.9 %copy-start.3 = (u32[256]{0:T(256)S(1)}, u32[256]{0:T(256)}, u32[]{:S(2)}) copy-start(u32[256]{0:T(256)} %constant.134) | copy-start | bytes 3076
  65.6 158.2 %copy-start.1 = (f32[96,256]{1,0:T(8,128)S(1)}, f32[96,256]{1,0:T(8,128)}, u32[]{:S(2)}) copy-start(f32[96,256]{1,0:T(8,128)} %param.8) | copy-start | bytes 294916
  292.7 1.2 copy-start
  293.9 165.7 %all-reduce.6.cloned.1.call-start = ((), (), s32[]{:S(2)}) async-start(), calls=%async_computation.2 | async-start | bytes 196608 | tf_op jit(solution)/shard_map/psum | solution.py:12
  365.0 295.9 %copy-start.2 = (f32[96,256]{1,0:T(8,128)}, f32[96,256]{1,0:T(8,128)S(1)}, u32[]{:S(2)}) copy-start(f32[96,256]{1,0:T(8,128)S(1)} %broadcast_multiply_fusion) | copy-start | bytes 294916
  365.9 201.0 %all-reduce.8.cloned.1.call-start = ((), (), s32[]{:S(2)}) async-start(), calls=%async_computation.3 | async-start | bytes 196608 | tf_op jit(solution)/shard_map/psum | solution.py:12
Sparse Core Ops, SparseCore 0:
  294.0 70.0 reduce-scatter.1
  368.0 91.5 all-reduce.5
  462.1 104.6 all-reduce.7

commit v2 on v0

--- a/solution.py
+++ b/solution.py
@@ -4,6 +4,12 @@
 from jax.sharding import PartitionSpec as P
 
 NEV = 32
+
+
+def summed_here(block, axis):
+    parts = lax.all_gather(block, axis, axis=0, tiled=False)
+    summed = parts.sum(axis=0)
+    return summed
 
 
 def step_width():
@@ -112,7 +118,7 @@
         precision=lax.Precision.HIGHEST,
         preferred_element_type=jnp.float32,
     )
-    residual_gram = lax.psum(local_r, ("row", "col")) / point_count
+    residual_gram = summed_here(local_r, ("row", "col")) / point_count
     factor_r = jnp.linalg.cholesky(residual_gram)
     q_block = jax.scipy.linalg.solve_triangular(factor_r, residual, lower=True)
     return (applied, gram_a, gram_b, q_block)

time: 712 us -> 751 us (1.055)
  waiting for transfers between devices: 316 us -> 427 us
  blocking collectives: 210 us -> 136 us
    all_gather x0 -> x1, waiting for transfers between devices: none -> 111 us  [summed_here(): parts = lax.all_gather(block, axis, axis=0, tiled=False)]
    psum x1 -> x0, blocking collectives: 74.3 us -> none  [per_device(): residual_gram = lax.psum(local_r, ('row', 'col')) / point_count]
  transfers between devices with their start and end apart: 2 -> 3, of which waited for: 2 -> 3; matrix products, arithmetic and copies ran while one was open for 0% -> 0% of each run, Pallas kernels for 0% -> 0%
where the time goes in v2:
time: 751 us; the launch traced here: 750 us
  waiting for transfers between devices  427 us (57%)
  blocking collectives  136 us (18%)
  matrix products  115 us (15%)
  local copies, waits for them, and re-layouts  39.3 us (5%)
  other arithmetic  17.9 us (2%)
  between operations  14.5 us (2%)
    psum x1, waiting for transfers between devices, per_device(): sum_a, sum_b = lax.psum((local_a, local_b), ('row', 'col'))  247 us
    all_gather x1, waiting for transfers between devices, summed_here(): parts = lax.all_gather(block, axis, axis=0, tiled=False)  111 us
    dot_general x16, matrix products, pair_tile(): lax.dot_general(source_points, target_points, (((0,), (0,)), ((), ())), p...  73.7 us
    reduce_scatter x1, waiting for transfers between devices, per_device(): lax.psum_scatter(totals, 'col', scatter_dimension=1, tiled=True)  69.3 us
    unnamed x1, blocking collectives  58.1 us
    dot_general x16, matrix products, accumulate_add_block(): jnp.dot(columns, tile_rows, preferred_element_type=jnp.float32)  37.7 us
    all_gather x1, blocking collectives, per_device(): lax.all_gather(scaled, 'row', axis=1, tiled=True)  30.7 us
    all_gather x1, blocking collectives, per_device(): source_points = lax.all_gather(points, 'row', axis=1, tiled=True)  27.3 us
  transfers between devices with their start and end apart: 3, of which 3 were waited for; matrix products, arithmetic and copies ran while one was open for 0% of the time, Pallas kernels for 0%

profile of v2, /device:TPU:1, one launch (start us, length us, event | category | flops | bytes accessed | tf_op | source)
XLA Modules:
  0.0 750.3 jit_solution(5840290401111498680)
XLA Ops:
  7.2 20.0 %all_gather.16 = f32[32,4096]{1,0:T(8,128)S(1)} all-gather(f32[32,256]{1,0:T(8,128)} %param.7), channel_id=1, replica_groups=mesh['row'=16,'col'=16] {'col'}, dimensions={1}, use_global_device_ids=true | all-gather | bytes 557056 | tf_op jit(solution)/shard_map/all_gather | solution.py:81
  27.2 27.3 %all_gather.15 = f32[32,4096]{1,0:T(8,128)S(1)} all-gather(f32[32,256]{1,0:T(8,128)} %param.7), channel_id=1, replica_groups=mesh['row'=16,'col'=16] {'row'}, dimensions={1}, use_global_device_ids=true | all-gather | bytes 557056 | tf_op jit(solution)/shard_map/all_gather | solution.py:82
  54.6 11.0 %broadcast_in_dim.20 = bf16[4096,4096]{1,0:T(8,128)(2,1)} broadcast(bf16[]{:T(256)} %constant.130.clone.1), dimensions={} | broadcast | bytes 33554432 | tf_op jit(solution)/shard_map/broadcast_in_dim | solution.py:48
  65.6 98.8 %while.30 = (s32[]{:T(128)}, f32[4096]{0:T(1024)S(1)}, bf16[4096,4096]{1,0:T(8,128)(2,1)}, f32[4096]{0:T(1024)S(1)}, f32[4096]{0:T(1024)S(1)}, /*index=5*/f32[32...) while((s32[]{:T(128)}, f32[4096]{0:T(1024)S(1)}, ...), condition=%wide.region_4.0_spmd.clone, body=%wide.region_2.0_spmd.clone.sunk | while | flops 408948736 | bytes 6933681 | solution.py:49
  65.6 4.6 fusion.40
  71.8 4.6 fusion.40
  78.0 4.6 fusion.40
  84.1 4.6 fusion.40
  96.5 4.6 fusion.40
  102.7 4.6 fusion.40
  108.9 4.6 fusion.40
  115.0 4.6 fusion.40
  121.2 4.6 fusion.40
  127.4 4.6 fusion.40
  133.5 4.6 fusion.40
  139.7 4.6 fusion.40
  145.9 4.6 fusion.40
  158.3 4.6 fusion.40
  164.3 58.1 %all-reduce = f32[4096]{0:T(1024)S(1)} all-reduce(f32[4096]{0:T(1024)S(1)} %get-tuple-element.209), channel_id=3, replica_groups=mesh['row'=16,'col'=16] {'col'}, use_global_device_ids=true, to_apply=%region_5.0.clone | all-reduce | flops 4096 | bytes 32768
  223.8 30.7 %all_gather.17 = bf16[96,4096]{1,0:T(8,128)(2,1)S(1)} all-gather(bf16[96,256]{1,0:T(8,128)(2,1)S(1)} %multiply_convert_fusion), channel_id=1, replica_groups=mesh['row'=16,'col'=16] {'row'}, dimensions={1}, use_global_device_ids=true | all-gather | bytes 835584 | tf_op jit(solution)/shard_map/all_gather | solution.py:88
  254.5 38.2 %while.31 = (s32[]{:T(128)}, f32[96,4096]{1,0:T(8,128)S(1)}, bf16[96,4096]{1,0:T(8,128)(2,1)S(1)}, bf16[4096,4096]{1,0:T(8,128)(2,1)}, s32[]{:T(128)}, /*index=5*/s32[]{:T(128)}, s32[]{:T(128)}, s32[]{:T(128)}) while((s32[]{:T(128)}, f32[96,4096]{1,0:T(8,128)S(1)}, bf16[96,4096]{1,0:T(8,128)(2,1)S(1)}, ...), condition=%wide.region_7.0_spmd.clone, body=%wide.region_6.0_spmd.clone.sunk | while | flops 202113024 | bytes 5293708 | solution.py:64
  294.8 69.3 %reduce-scatter.2.cloned.1.call-done = f32[96,256]{1,0:T(8,128)} async-done(((f32[96,4096]{1,0:T(8,128)}), f32[96,256]{1,0:T(8,128)}) %reduce-scatter.2.cloned.1.call-update) | async-done | bytes 98320 | tf_op jit(solution)/shard_map/reduce_scatter | solution.py:90
  365.9 246.6 %all-reduce.4.cloned.1.call-done = (f32[96,96]{0,1:T(8,128)}, f32[96,96]{0,1:T(8,128)}) async-done(((f32[96,96]{0,1:T(8,128)}, f32[96,96]{0,1:T(8,128)}), (f32[96,96]{0,1:T(8,128)}, f32[96,96]{0,1:T(8,128)})) %all-reduce.4.cloned.1.call-update) | async-done | bytes 73744 | tf_op jit(solution)/shard_map/psum | solution.py:108
  622.9 110.6 %all-gather.3.cloned.1.call-done = f32[8192,32]{1,0:T(8,128)} async-done(((f32[32,32]{1,0:T(8,128)}), f32[8192,32]{1,0:T(8,128)}) %all-gather.3.cloned.1.call-update) | async-done | bytes 1048592 | tf_op jit(solution)/shard_map/all_gather | solution.py:10
  (116 shorter events, 97.2 us)
Async XLA Ops:
  7.2 356.9 %reduce-scatter.2.cloned.1.call-start = ((), (), s32[]{:S(2)}) async-start(), calls=%async_computation.1 | async-start | bytes 1671168 | tf_op jit(solution)/shard_map/reduce_scatter | solution.py:90
  65.6 156.9 %copy-start.3 = (u32[256]{0:T(256)S(1)}, u32[256]{0:T(256)}, u32[]{:S(2)}) copy-start(u32[256]{0:T(256)} %constant.134) | copy-start | bytes 3076
  65.6 158.2 %copy-start.1 = (f32[96,256]{1,0:T(8,128)S(1)}, f32[96,256]{1,0:T(8,128)}, u32[]{:S(2)}) copy-start(f32[96,256]{1,0:T(8,128)} %param.8) | copy-start | bytes 294916
  292.7 1.2 copy-start
  293.9 318.6 %all-reduce.4.cloned.1.call-start = ((), (), s32[]{:S(2)}) async-start(), calls=%async_computation.3 | async-start | bytes 196608 | tf_op jit(solution)/shard_map/psum | solution.py:108
  365.0 378.8 %copy-start.2 = (f32[96,256]{1,0:T(8,128)}, f32[96,256]{1,0:T(8,128)S(1)}, u32[]{:S(2)}) copy-start(f32[96,256]{1,0:T(8,128)S(1)} %broadcast_multiply_fusion) | copy-start | bytes 294916
  365.9 367.7 %all-gather.3.cloned.1.call-start = ((), (), s32[]{:S(2)}) async-start(), calls=%async_computation.2 | async-start | bytes 4210688 | tf_op jit(solution)/shard_map/all_gather | solution.py:10
Sparse Core Ops, SparseCore 0:
  294.0 70.0 reduce-scatter.1
  370.3 242.1 all-reduce.3
  621.6 111.8 all-gather.2
